TPU v7x, 32 devices: a whole 2x2x4 slice. The times are simulated.
32 devices in a mesh: aux: 4 (over z), pair: 8 (over y, x, core).
Axes of the slice: x: 2, y: 2, z: 4, core: 2. Of those that a mesh axis runs over, the one named last changes fastest.
Arguments:
- metric: bfloat16 [4096, 4096], P('aux', 'pair'), may hold values from -0.09375 to 0.09375
- amplitudes: bfloat16 [4096, 16384], P('aux', 'pair'), may hold values from -0.59765625 to 0.59765625
- virt_coef: bfloat16 [1024, 1280], replicated, may hold values from -1.5 to 1.5
Outputs:
- density: float32 [4096, 4096], P('aux', 'pair')
- fitted_ao: bfloat16 [4096, 20480], P(('aux', 'pair'))
All inputs are finite; a program needn't handle non-finite values.
Results may differ from a plain program's by a relative error of at most 0.012.
Values may be sent and summed in bfloat16 or wider, within the bound.
A program may use at most 128 MiB of HBM per device.

v0:
```python
import jax
import jax.numpy as jnp
from jax import lax
from jax.sharding import PartitionSpec as P


def shards(metric, amplitudes, virt_coef):
    rows_metric = lax.all_gather(metric, "pair", axis=1, tiled=True)
    full_amp = lax.all_gather(amplitudes, "aux", axis=0, tiled=True)
    fitted = jnp.dot(rows_metric, full_amp, preferred_element_type=jnp.float32).astype(jnp.bfloat16)
    partial_value = lax.dot_general(
        fitted, full_amp, (((1,), (1,)), ((), ())), preferred_element_type=jnp.float32
    )
    density = lax.psum_scatter(
        partial_value.astype(jnp.bfloat16), "pair", scatter_dimension=1, tiled=True
    ).astype(jnp.float32)
    regrouped = lax.all_to_all(fitted, "pair", split_axis=0, concat_axis=1, tiled=True)
    row_count = regrouped.shape[0]
    virt_count = virt_coef.shape[0]
    ao_count = virt_coef.shape[1]
    occ_count = regrouped.shape[1] // virt_count
    blocks = regrouped.reshape(row_count * occ_count, virt_count)
    fitted_ao = jnp.dot(blocks, virt_coef, preferred_element_type=jnp.float32).astype(jnp.bfloat16)
    return (density, fitted_ao.reshape(row_count, occ_count * ao_count))


def solution(mesh):
    in_specs = (P("aux", "pair"), P("aux", "pair"), P())
    out_specs = (P("aux", "pair"), P(("aux", "pair"), None))
    return jax.shard_map(shards, mesh=mesh, in_specs=in_specs, out_specs=out_specs, check_vma=False)
```

profile of v0, /device:TPU:0, one launch (start us, length us, event | category | flops | bytes accessed | tf_op | source)
XLA Modules:
  0.0 516.1 jit_solution(2569435131899505442)
XLA Ops:
  7.2 0.0 copy-start
  7.2 0.0 all-gather.3.cloned.1.call-start
  7.2 0.7 all-gather.3.cloned.1.call-update
  7.9 0.0 all-gather.5.cloned.1.call-start
  8.0 0.7 all-gather.5.cloned.1.call-update
  8.7 0.0 reduce-scatter.2.cloned.1.call-start
  8.7 59.8 %all-gather.3.cloned.1.call-done = bf16[1024,4096]{1,0:T(8,128)(2,1)} async-done(((bf16[1024,512]{1,0:T(8,128)(2,1)}), bf16[1024,4096]{1,0:T(8,128)(2,1)}) %all-gather.3.cloned.1.call-update) | async-done | bytes 8388624 | tf_op jit(solution)/shard_map/all_gather | solution.py:8
  68.5 288.4 %all-gather.5.cloned.1.call-done = bf16[4096,2048]{1,0:T(8,128)(2,1)} async-done(((bf16[1024,2048]{1,0:T(8,128)(2,1)}), bf16[4096,2048]{1,0:T(8,128)(2,1)}) %all-gather.5.cloned.1.call-update) | async-done | bytes 16777232 | tf_op jit(solution)/shard_map/all_gather | solution.py:9
  356.8 0.0 copy-start.2
  356.8 22.8 %fusion.1 = bf16[1024,2048]{1,0:T(8,128)(2,1)S(1)} fusion(bf16[1024,4096]{1,0:T(8,128)(2,1)} %all-gather.3.cloned.1.call-done, bf16[4096,2048]{1,0:T(8,128)(2,1)} %all-gather.5.cloned.1.call-done), kind=kOutput, calls=%fused_computation.3 | convolution fusion | flops 17179869184 | bytes 29360128 | tf_op jit(solution)/shard_map/dot_general | solution.py:10
  379.7 0.0 copy-start.1
  379.7 2.0 copy-done.1
  381.7 0.0 copy-done.2
  381.7 19.6 %convolution_convert_fusion.1 = bf16[1024,4096]{1,0:T(8,128)(2,1)} fusion(bf16[4096,2048]{1,0:T(8,128)(2,1)S(1)} %copy-done.2, bf16[1024,2048]{1,0:T(8,128)(2,1)S(1)} %fusion.1), kind=kOutput, calls=%fused_computation.1 | convolution fusion | flops 17184063488 | bytes 29360128 | tf_op jit(solution)/shard_map/dot_general | solution.py:11
  401.2 0.0 reduce-scatter.2.cloned.1.call-update
  401.3 75.2 %all_to_all.16 = bf16[8,128,2048]{2,1,0:T(8,128)(2,1)S(1)} all-to-all(bf16[8,128,2048]{2,1,0:T(8,128)(2,1)} %bitcast.9), channel_id=1, replica_groups=mesh['aux'=4,'pair'=8] {'pair'}, dimensions={0} | all-to-all | bytes 8388608 | tf_op jit(solution)/shard_map/all_to_all | solution.py:17
  476.4 4.4 copy.6
  480.8 7.1 %reshape.14 = bf16[2048,1024]{1,0:T(8,128)(2,1)} reshape(bf16[128,8,2048]{2,1,0:T(8,128)(2,1)} %copy.6) | data formatting | bytes 8388608 | tf_op jit(solution)/shard_map/reshape | solution.py:22
  487.9 0.0 copy-done
  487.9 10.8 %convolution_convert_fusion = bf16[2048,1280]{1,0:T(8,128)(2,1)} fusion(bf16[2048,1024]{1,0:T(8,128)(2,1)} %reshape.14, bf16[1024,1280]{1,0:T(8,128)(2,1)S(1)} %copy-done), kind=kOutput, calls=%fused_computation | convolution fusion | flops 5371330560 | bytes 12058624 | tf_op jit(solution)/shard_map/dot_general | solution.py:23
  498.7 8.1 %reshape.15 = bf16[128,20480]{1,0:T(8,128)(2,1)} reshape(bf16[2048,1280]{1,0:T(8,128)(2,1)} %convolution_convert_fusion) | data formatting | bytes 10485760 | tf_op jit(solution)/shard_map/reshape | solution.py:24
  506.7 0.0 reduce-scatter.2.cloned.1.call-done
  506.7 2.8 convert_element_type.14
Async XLA Ops:
  7.2 480.7 %copy-start = (bf16[1024,1280]{1,0:T(8,128)(2,1)S(1)}, bf16[1024,1280]{1,0:T(8,128)(2,1)}, u32[]{:S(2)}) copy-start(bf16[1024,1280]{1,0:T(8,128)(2,1)} %param.5) | copy-start | bytes 7864324
  7.2 61.3 %all-gather.3.cloned.1.call-start = ((), (), s32[]{:S(2)}) async-start(), calls=%async_computation.2 | async-start | bytes 9437184 | tf_op jit(solution)/shard_map/all_gather | solution.py:8
  7.9 348.9 %all-gather.5.cloned.1.call-start = ((), (), s32[]{:S(2)}) async-start(), calls=%async_computation.3 | async-start | bytes 20971520 | tf_op jit(solution)/shard_map/all_gather | solution.py:9
  8.7 498.0 %reduce-scatter.2.cloned.1.call-start = ((), (), s32[]{:S(2)}) async-start(), calls=%async_computation.4 | async-start | bytes 9437184 | tf_op jit(solution)/shard_map/reduce_scatter | solution.py:14
  356.8 24.9 %copy-start.2 = (bf16[4096,2048]{1,0:T(8,128)(2,1)S(1)}, bf16[4096,2048]{1,0:T(8,128)(2,1)}, u32[]{:S(2)}) copy-start(bf16[4096,2048]{1,0:T(8,128)(2,1)} %all-gather.5.cloned.1.call-done) | copy-start | bytes 50331652
  379.7 2.0 copy-start.1
Sparse Core Ops, SparseCore 0:
  9.9 58.5 all-gather.2
  70.0 286.7 all-gather.4
  401.4 92.9 reduce-scatter.1
where the time goes:
time: 517 us; the launch traced here: 516 us
  waiting for transfers between devices  350 us (68%)
  blocking collectives  75.2 us (15%)
  matrix products  53.1 us (10%)
  local copies, waits for them, and re-layouts  21.5 us (4%)
  between operations  13.8 us (3%)
    all_gather x1, waiting for transfers between devices, shards(): full_amp = lax.all_gather(amplitudes, 'aux', axis=0, tiled=True)  288 us
    all_to_all x1, blocking collectives, shards(): lax.all_to_all(fitted, 'pair', split_axis=0, concat_axis=1, tiled=True)  75.2 us
    all_gather x1, waiting for transfers between devices, shards(): rows_metric = lax.all_gather(metric, 'pair', axis=1, tiled=True)  59.8 us
    dot_general x1, matrix products, shards(): jnp.dot(rows_metric, full_amp, preferred_element_type=jnp.float32)  22.8 us
    dot_general x1, matrix products, shards(): lax.dot_general(fitted, full_amp, (((1,), (1,)), ((), ())), preferred_ele...  19.6 us
    dot_general x1, matrix products, shards(): jnp.dot(blocks, virt_coef, preferred_element_type=jnp.float32)  10.8 us
  transfers between devices with their start and end apart: 3, of which 2 were waited for; matrix products, arithmetic and copies ran while one was open for 6% of the time, Pallas kernels for 0%

commit v1 on v0

--- a/solution.py
+++ b/solution.py
@@ -4,9 +4,20 @@
 from jax.sharding import PartitionSpec as P
 
 
+def gather_by_hops(x, name, dim):
+    n_dev = lax.axis_size(name)
+    hops = [(i, (i + 1) % n_dev) for i in range(n_dev)]
+    pieces = [x]
+    for reach in range(1, n_dev):
+        pieces = [lax.ppermute(pieces[0], name, hops), *pieces]
+    full = jnp.concatenate(pieces, axis=dim)
+    offset = (lax.axis_index(name) + 1) * pieces[-1].shape[dim]
+    return jnp.roll(full, offset, axis=dim)
+
+
 def shards(metric, amplitudes, virt_coef):
     rows_metric = lax.all_gather(metric, "pair", axis=1, tiled=True)
-    full_amp = lax.all_gather(amplitudes, "aux", axis=0, tiled=True)
+    full_amp = gather_by_hops(amplitudes, "aux", 0)
     fitted = jnp.dot(rows_metric, full_amp, preferred_element_type=jnp.float32).astype(jnp.bfloat16)
     partial_value = lax.dot_general(
         fitted, full_amp, (((1,), (1,)), ((), ())), preferred_element_type=jnp.float32

time: 517 us -> 486 us (0.940)
  waiting for transfers between devices: 350 us -> 280 us
  local copies, waits for them, and re-layouts: 21.5 us -> 54.6 us
    all_gather x1 -> x0, waiting for transfers between devices: 288 us -> none  [shards(): full_amp = lax.all_gather(amplitudes, 'aux', axis=0, tiled=True)]
    ppermute x0 -> x3, waiting for transfers between devices: none -> 280 us  [gather_by_hops(): pieces = [lax.ppermute(pieces[0], name, hops), *pieces]]
    all_gather x1, waiting for transfers between devices: 59.8 us -> 0.01 us  [shards(): rows_metric = lax.all_gather(metric, 'pair', axis=1, tiled=True)]
    unnamed x6 -> x13, local copies, waits for them, and re-layouts: 2.02 us -> 32.8 us
  transfers between devices with their start and end apart: 3 -> 5, of which waited for: 2 -> 3; matrix products, arithmetic and copies ran while one was open for 6% -> 13% of each run, Pallas kernels for 0% -> 0%
where the time goes in v1:
time: 486 us; the launch traced here: 485 us
  waiting for transfers between devices  280 us (58%)
  blocking collectives  75.1 us (15%)
  matrix products  55.2 us (11%)
  local copies, waits for them, and re-layouts  54.6 us (11%)
  between operations  14.1 us (3%)
    ppermute x3, waiting for transfers between devices, gather_by_hops(): pieces = [lax.ppermute(pieces[0], name, hops), *pieces]  280 us
    all_to_all x1, blocking collectives, shards(): lax.all_to_all(fitted, 'pair', split_axis=0, concat_axis=1, tiled=True)  75.1 us
    unnamed x13, local copies, waits for them, and re-layouts  32.8 us
    dot_general x1, matrix products, shards(): jnp.dot(rows_metric, full_amp, preferred_element_type=jnp.float32)  22.7 us
    dot_general x1, matrix products, shards(): lax.dot_general(fitted, full_amp, (((1,), (1,)), ((), ())), preferred_ele...  21.7 us
    dot_general x1, matrix products, shards(): jnp.dot(blocks, virt_coef, preferred_element_type=jnp.float32)  10.8 us
  transfers between devices with their start and end apart: 5, of which 3 were waited for; matrix products, arithmetic and copies ran while one was open for 13% of the time, Pallas kernels for 0%

profile of v1, /device:TPU:0, one launch (start us, length us, event | category | flops | bytes accessed | tf_op | source)
XLA Modules:
  0.0 484.7 jit_solution(10569450406399106259)
XLA Ops:
  7.2 0.0 all-gather.2.cloned.1.call-start
  7.2 3.1 collective-permute-start
  10.3 0.0 all-gather.2.cloned.1.call-update
  10.4 0.0 reduce-scatter.2.cloned.1.call-start
  10.4 92.8 %collective-permute-done = bf16[1024,2048]{1,0:T(8,128)(2,1)} collective-permute-done((bf16[1024,2048]{1,0:T(8,128)(2,1)}, bf16[1024,2048]{1,0:T(8,128)(2,1)}, u32[]{:S(2)}, u32[]{:S(2)}) %collective-permute-start) | collective-permute-done | bytes 4194336 | tf_op jit(solution)/shard_map/ppermute | solution.py:12
  103.2 93.8 %collective-permute-done.1 = bf16[1024,2048]{1,0:T(8,128)(2,1)} collective-permute-done((bf16[1024,2048]{1,0:T(8,128)(2,1)}, bf16[1024,2048]{1,0:T(8,128)(2,1)}, u32[]{:S(2)}, u32[]{:S(2)}) %collective-permute-start.1) | collective-permute-done | bytes 4194336 | tf_op jit(solution)/shard_map/ppermute | solution.py:12
  197.1 93.0 %collective-permute-done.2 = bf16[1024,2048]{1,0:T(8,128)(2,1)} collective-permute-done((bf16[1024,2048]{1,0:T(8,128)(2,1)}, bf16[1024,2048]{1,0:T(8,128)(2,1)}, u32[]{:S(2)}, u32[]{:S(2)}) %collective-permute-start.2) | collective-permute-done | bytes 4194336 | tf_op jit(solution)/shard_map/ppermute | solution.py:12
  290.1 4.7 constant_dynamic-update-slice_fusion.7
  294.8 4.9 %constant_dynamic-update-slice_fusion.6 = bf16[8192,2048]{1,0:T(8,128)(2,1)} fusion(bf16[8192,2048]{1,0:T(8,128)(2,1)} %constant_dynamic-update-slice_fusion.7, bf16[1024,2048]{1,0:T(8,128)(2,1)} %collective-permute-done.1), kind=kLoop, calls=%fused_computation.13 | loop fusion | bytes 8388608
  299.7 4.7 constant_dynamic-update-slice_fusion.5
  304.5 2.2 constant_dynamic-update-slice_fusion.4
  306.7 4.7 constant_dynamic-update-slice_fusion.3
  311.4 4.7 constant_dynamic-update-slice_fusion.2
  316.2 4.7 constant_dynamic-update-slice_fusion.1
  320.9 2.2 constant_dynamic-update-slice_fusion
  323.1 22.7 %fusion.2 = bf16[2048,1024]{0,1:T(8,128)(2,1)S(1)} fusion(bf16[1024,4096]{1,0:T(8,128)(2,1)} %all-gather.2.cloned.1.call-done, bf16[8192,2048]{1,0:T(8,128)(2,1)} %constant_dynamic-update-slice_fusion, s32[]{:T(128)S(6)} %select_n.14), kind=kOutput, calls=%fused_computation.2 | convolution fusion | flops 17179869184 | bytes 29360132 | tf_op jit(solution)/shard_map/dot_general | solution.py:21
  345.8 2.0 copy-done.2
  347.8 21.7 %fusion.4 = bf16[1024,4096]{1,0:T(8,128)(2,1)} fusion(bf16[8192,2048]{1,0:T(8,128)(2,1)} %constant_dynamic-update-slice_fusion, s32[]{:T(128)S(6)} %select_n.14, bf16[2048,1024]{0,1:T(8,128)(2,1)S(1)} %fusion.2), kind=kOutput, calls=%fused_computation.4 | convolution fusion | flops 17184063488 | bytes 29360132 | tf_op jit(solution)/shard_map/dot_general | solution.py:22
  369.6 75.1 %all_to_all.16 = bf16[8,128,2048]{2,1,0:T(8,128)(2,1)S(1)} all-to-all(bf16[8,128,2048]{2,1,0:T(8,128)(2,1)} %bitcast.9), channel_id=1, replica_groups=mesh['aux'=4,'pair'=8] {'pair'}, dimensions={0} | all-to-all | bytes 8388608 | tf_op jit(solution)/shard_map/all_to_all | solution.py:28
  444.7 4.3 copy.6
  449.0 7.2 %reshape.14 = bf16[2048,1024]{1,0:T(8,128)(2,1)} reshape(bf16[128,8,2048]{2,1,0:T(8,128)(2,1)} %copy.6) | data formatting | bytes 8388608 | tf_op jit(solution)/shard_map/reshape | solution.py:33
  456.2 10.8 %convolution_convert_fusion = bf16[2048,1280]{1,0:T(8,128)(2,1)} fusion(bf16[2048,1024]{1,0:T(8,128)(2,1)} %reshape.14, bf16[1024,1280]{1,0:T(8,128)(2,1)S(1)} %copy-done), kind=kOutput, calls=%fused_computation.5 | convolution fusion | flops 5371330560 | bytes 12058624 | tf_op jit(solution)/shard_map/dot_general | solution.py:34
  467.0 8.1 %reshape.15 = bf16[128,20480]{1,0:T(8,128)(2,1)} reshape(bf16[2048,1280]{1,0:T(8,128)(2,1)} %convolution_convert_fusion) | data formatting | bytes 10485760 | tf_op jit(solution)/shard_map/reshape | solution.py:35
  475.1 2.8 convert_element_type.17
  (10 shorter events, 0.0 us)
Async XLA Ops:
  7.2 449.1 %copy-start = (bf16[1024,1280]{1,0:T(8,128)(2,1)S(1)}, bf16[1024,1280]{1,0:T(8,128)(2,1)}, u32[]{:S(2)}) copy-start(bf16[1024,1280]{1,0:T(8,128)(2,1)} %param.5) | copy-start | bytes 7864324
  7.2 316.0 %all-gather.2.cloned.1.call-start = ((), (), s32[]{:S(2)}) async-start(), calls=%async_computation.2 | async-start | bytes 9437184 | tf_op jit(solution)/shard_map/all_gather | solution.py:19
  7.2 96.0 %collective-permute-start = (bf16[1024,2048]{1,0:T(8,128)(2,1)}, bf16[1024,2048]{1,0:T(8,128)(2,1)}, u32[]{:S(2)}, u32[]{:S(2)}) collective-permute-start(bf16[1024,2048]{1,0:T(8,128)(2,1)} %param.4), channel_id=1, source_target_pairs={{0,8},{8,16},{16,24},{24,0},{1,9},{9,17},{17,25},{25,1},{2,10},{10... | collective-permute-start | bytes 12582920 | tf_op jit(solution)/shard_map/ppermute | solution.py:12
  10.4 464.7 %reduce-scatter.2.cloned.1.call-start = ((), (), s32[]{:S(2)}) async-start(), calls=%async_computation.3 | async-start | bytes 9437184 | tf_op jit(solution)/shard_map/reduce_scatter | solution.py:25
  103.2 93.8 %collective-permute-start.1 = (bf16[1024,2048]{1,0:T(8,128)(2,1)}, bf16[1024,2048]{1,0:T(8,128)(2,1)}, u32[]{:S(2)}, u32[]{:S(2)}) collective-permute-start(bf16[1024,2048]{1,0:T(8,128)(2,1)} %collective-permute-done), channel_id=1, source_target_pairs={{0,8},{8,16},{16,24},{24,0},{1,9},{9,17},{17,25},{25,1},{2,10},{10... | collective-permute-start | bytes 12582920 | tf_op jit(solution)/shard_map/ppermute | solution.py:12
  197.1 93.0 %collective-permute-start.2 = (bf16[1024,2048]{1,0:T(8,128)(2,1)}, bf16[1024,2048]{1,0:T(8,128)(2,1)}, u32[]{:S(2)}, u32[]{:S(2)}) collective-permute-start(bf16[1024,2048]{1,0:T(8,128)(2,1)} %collective-permute-done.1), channel_id=1, source_target_pairs={{0,8},{8,16},{16,24},{24,0},{1,9},{9,17},{17,25},{25,1},{2,10},{10... | collective-permute-start | bytes 12582920 | tf_op jit(solution)/shard_map/ppermute | solution.py:12
  294.8 9.7 %copy-start.1 = (bf16[1024,2048]{1,0:T(8,128)(2,1)S(1)}, bf16[1024,2048]{1,0:T(8,128)(2,1)}, u32[]{:S(2)}) copy-start(bf16[1024,2048]{1,0:T(8,128)(2,1)} %param.4) | copy-start | bytes 12582916
  345.8 2.0 copy-start.2
Sparse Core Ops, SparseCore 0:
  10.5 57.9 all-gather.1
  369.7 92.8 reduce-scatter.1
